TPU v7x, 256 devices: a whole 4x4x8 slice. The times are simulated.
256 devices in a mesh: seq: 32 (over x, z), tp: 4 (over y), lat: 2 (over core).
Axes of the slice: x: 4, y: 4, z: 8, core: 2. Of those that a mesh axis runs over, the one named last changes fastest.
Arguments:
- tokens: bfloat16 [24576, 8192], P(('seq', 'lat'), 'tp'), may hold values from -6 to 6
- active: int32 [24576, 4], P(('seq', 'lat')), may hold values from 0 to 255, all different within a row; in each aligned block of 384 rows (0 to 383, 384 to 767, ...) at most 9 rows name the same one
- placement_map: int32 [256], replicated, may hold values from 0 to 255, each once
- enc_weight: bfloat16 [8192, 32768], P('tp', ('seq', 'lat')), may hold values from -0.0625 to 0.0625
- enc_bias: float32 [32768], P(('seq', 'lat')), may hold values from -3 to 3
- dec_weight: bfloat16 [32768, 8192], P(('seq', 'lat'), 'tp'), may hold values from -0.375 to 0.375
- dec_bias: float32 [8192], P('tp'), may hold values from -3 to 3
Outputs:
- recon: bfloat16 [24576, 8192], P(('seq', 'lat'), 'tp')
Inputs may be any that keep to these rules, and one draw needn't show every extreme that they name: `active`: the 4 blocks of one token are different. Among the rows of one device (aligned blocks of 384 rows) no block is named more than 9 times, and some block is named exactly 9 times. `placement_map`: each column block appears once.
All inputs are finite; a program needn't handle non-finite values.
Results may differ from a plain program's by a relative error of at most 0.0061.
Values may be sent and summed in bfloat16 or wider, within the bound.
A program may use at most 128 MiB of HBM per device.

v0:
```python
import jax
import jax.numpy as jnp
from jax import lax
from jax.sharding import PartitionSpec as P


def local(tokens, active, placement_map, enc_weight, enc_bias, dec_weight, dec_bias):
    rows, width = tokens.shape
    top = active.shape[1]
    nblocks = placement_map.shape[0]
    seq_count = lax.axis_size("seq")
    lat_count = lax.axis_size("lat")
    owners = seq_count * lat_count
    local_blocks = nblocks // owners
    block_width = enc_bias.shape[0] // local_blocks
    capacity = 3 * rows * top // (2 * nblocks)
    centered = (tokens.astype(jnp.float32) - dec_bias[None, :]).astype(jnp.bfloat16)
    block_ids = jnp.arange(nblocks, dtype=jnp.int32)
    matches = (active[:, :, None] == block_ids[None, None, :]).astype(jnp.int32)
    position = jnp.sum(matches * placement_map[None, None, :], axis=2).reshape(-1)
    pos_hot = (position[:, None] == block_ids[None, :]).astype(jnp.int32)
    rank = jnp.sum((jnp.cumsum(pos_hot, axis=0) - 1) * pos_hot, axis=1)
    target = position * capacity + rank
    pair_row = jnp.arange(rows * top, dtype=jnp.int32) // top
    slot_row = jnp.zeros((nblocks * capacity,), jnp.int32).at[target].set(pair_row)
    filled = jnp.zeros((nblocks * capacity,), jnp.bool_).at[target].set(True)
    outgoing = jnp.where(filled[:, None], centered[slot_row], jnp.zeros((), jnp.bfloat16))
    outgoing = outgoing.reshape(owners, local_blocks, capacity, width)
    enc_blocks = enc_weight.reshape(width, local_blocks, block_width)
    bias_blocks = enc_bias.reshape(local_blocks, block_width)
    dec_blocks = dec_weight.reshape(local_blocks, block_width, width)
    preact = jnp.einsum(
        "sbcd,dbh->sbch",
        lax.all_to_all(outgoing, ("seq", "lat"), split_axis=0, concat_axis=0, tiled=True),
        enc_blocks,
        preferred_element_type=jnp.float32,
    )
    summed = lax.psum(preact, "tp")
    codes = jnp.maximum(summed + bias_blocks[None, :, None, :], 0.0).astype(jnp.bfloat16)
    returned = lax.all_to_all(
        jnp.einsum("sbch,bhd->sbcd", codes, dec_blocks, preferred_element_type=jnp.float32).astype(
            jnp.bfloat16
        ),
        ("seq", "lat"),
        split_axis=0,
        concat_axis=0,
        tiled=True,
    )
    returned = returned.reshape(nblocks * capacity, width)
    contrib = returned[target].reshape(rows, top, width).astype(jnp.float32)
    return (jnp.sum(contrib, axis=1) + dec_bias[None, :]).astype(jnp.bfloat16)


def solution(mesh):
    return jax.shard_map(
        local,
        mesh=mesh,
        in_specs=(
            P(("seq", "lat"), "tp"),
            P(("seq", "lat"), None),
            P(),
            P("tp", ("seq", "lat")),
            P(("seq", "lat")),
            P(("seq", "lat"), "tp"),
            P("tp"),
        ),
        out_specs=P(("seq", "lat"), "tp"),
        check_vma=False,
    )
```

profile of v0, /device:TPU:4, one launch (start us, length us, event | category | flops | bytes accessed | tf_op | source)
XLA Modules:
  0.0 685.1 jit_solution(1939051492768150350)
XLA Ops:
  6.5 1.4 select_reduce_fusion
  8.0 0.1 eq.45
  8.5 0.3 fusion.3
  8.8 1.3 copy-done.2
  10.2 1.8 add_add_fusion
  12.1 2.1 copy.32
  14.3 0.2 mul.31
  14.4 1.9 fusion.5
  16.4 6.4 scatter_custom_fusion.1
  22.8 2.9 subtract_convert_fusion
  25.7 20.0 %gather_fusion = bf16[2304,2048]{1,0:T(8,128)(2,1)} fusion(bf16[384,2048]{1,0:T(8,128)(2,1)} %subtract_convert_fusion, s32[3072]{0:T(1024)S(1)} %pad_clamp_fusion), kind=kCustom, calls=%fused_computation | custom fusion | bytes 18883584 | tf_op jit(solution)/shard_map/gather | solution.py:27
  45.7 15.1 %gather.9 = bf16[64,4,9,2048]{3,2,1,0:T(8,128)(2,1)} reshape(bf16[2304,2048]{1,0:T(8,128)(2,1)} %gather_fusion) | data formatting | bytes 18874368 | tf_op jit(solution)/shard_map/gather | solution.py:27
  60.8 11.2 %scatter_custom_fusion = pred[2304]{0:T(1024)(128)(4,1)S(1)} fusion(s32[1536]{0:T(1024)S(1)} %fusion.17, pred[1536]{0:T(1024)(128)(4,1)S(1)} %broadcast.82, pred[]{:T(512)} %constant.16.clone.1), kind=kCustom, calls=%fused_computation.40 | custom fusion | bytes 2305 | tf_op jit(solution)/shard_map/scatter | solution.py:26
  72.0 0.2 broadcast_in_dim.35
  72.2 8.3 %broadcast_select_fusion = bf16[64,4,9,2048]{3,2,1,0:T(8,128)(2,1)S(1)} fusion(bf16[64,4,9,2048]{3,2,1,0:T(8,128)(2,1)} %gather.9, pred[64,4,9]{2,1,0:T(4,128)(4,1)S(1)} %broadcast_in_dim.35), kind=kLoop, calls=%fused_computation.4 | loop fusion | flops 4718592 | bytes 18876672 | tf_op jit(solution)/shard_map/jit(_where)/select_n | solution.py:27
  80.5 19.6 %copy.33 = bf16[64,4,9,2048]{3,1,2,0:T(4,128)(2,1)} copy(bf16[64,4,9,2048]{3,2,1,0:T(8,128)(2,1)S(1)} %broadcast_select_fusion) | data formatting | bytes 18874368 | tf_op jit(solution)/shard_map/jit(_where)/select_n | solution.py:27
  100.1 12.3 %all-to-all-start = ((bf16[64,4,9,2048]{3,1,2,0:T(4,128)(2,1)}), bf16[64,4,9,2048]{3,1,2,0:T(4,128)(2,1)}, u32[]{:S(2)}, u32[]{:S(2)}) async-start(bf16[64,4,9,2048]{3,1,2,0:T(4,128)(2,1)} %copy.33), calls=%async_computation | async-start | bytes 18874368 | tf_op jit(solution)/shard_map/all_to_all | solution.py:34
  112.3 0.3 all-reduce.2.cloned.1.call-start
  112.6 4.0 reshape.73
  116.6 200.8 %all-to-all-done = bf16[64,4,9,2048]{3,1,2,0:T(4,128)(2,1)} async-done(((bf16[64,4,9,2048]{3,1,2,0:T(4,128)(2,1)}), bf16[64,4,9,2048]{3,1,2,0:T(4,128)(2,1)}, u32[]{:S(2)}, u32[]{:S(2)}) %all-to-all-start) | async-done | bytes 9437216 | tf_op jit(solution)/shard_map/all_to_all | solution.py:34
  317.3 10.5 %fusion.6 = f32[64,4,9,128]{3,0,2,1:T(8,128)} fusion(bf16[2048,4,128,1]{2,1,0,3:T(4,128)(2,1)} %bitcast.22, bf16[64,4,9,2048]{3,1,2,0:T(4,128)(2,1)} %all-to-all-done), kind=kOutput, calls=%fused_computation.20 | convolution fusion | flops 1207959552 | bytes 12713984 | tf_op jit(solution)/shard_map/sbcd,dbh->sbch/dot_general | solution.py:32
  327.9 51.9 %all-reduce.2.cloned.1.call-done = f32[64,4,9,128]{3,0,2,1:T(8,128)} async-done(((f32[64,4,9,128]{3,0,2,1:T(8,128)}), f32[64,4,9,128]{3,0,2,1:T(8,128)}) %all-reduce.2.cloned.1.call-update) | async-done | bytes 1179664 | tf_op jit(solution)/shard_map/psum | solution.py:38
  379.7 4.1 convert_bitcast_fusion
  383.8 7.3 %copy.36 = bf16[64,4,9,2048]{3,1,2,0:T(4,128)(2,1)} copy(bf16[64,4,9,2048]{3,0,2,1:T(8,128)(2,1)S(1)} %convert_bitcast_fusion) | data formatting | bytes 18874368 | tf_op jit(solution)/shard_map/convert_element_type | solution.py:41
  391.2 10.8 %all-to-all-start.1 = ((bf16[64,4,9,2048]{3,1,2,0:T(4,128)(2,1)}), bf16[64,4,9,2048]{3,1,2,0:T(4,128)(2,1)}, u32[]{:S(2)}, u32[]{:S(2)}) async-start(bf16[64,4,9,2048]{3,1,2,0:T(4,128)(2,1)} %copy.36), calls=%async_computation.1 | async-start | bytes 18874368 | tf_op jit(solution)/shard_map/all_to_all | solution.py:40
  402.0 205.0 %all-to-all-done.1 = bf16[64,4,9,2048]{3,1,2,0:T(4,128)(2,1)} async-done(((bf16[64,4,9,2048]{3,1,2,0:T(4,128)(2,1)}), bf16[64,4,9,2048]{3,1,2,0:T(4,128)(2,1)}, u32[]{:S(2)}, u32[]{:S(2)}) %all-to-all-start.1) | async-done | bytes 9437216 | tf_op jit(solution)/shard_map/all_to_all | solution.py:40
  607.0 10.7 %copy.37 = bf16[64,4,9,2048]{3,2,1,0:T(8,128)(2,1)} copy(bf16[64,4,9,2048]{3,1,2,0:T(4,128)(2,1)} %all-to-all-done.1) | data formatting | bytes 18874368 | tf_op jit(solution)/shard_map/all_to_all | solution.py:40
  617.7 15.8 %reshape.75 = bf16[2304,2048]{1,0:T(8,128)(2,1)} reshape(bf16[64,4,9,2048]{3,2,1,0:T(8,128)(2,1)} %copy.37) | data formatting | bytes 18874368 | tf_op jit(solution)/shard_map/reshape | solution.py:49
  633.5 17.6 %gather_fusion.1 = bf16[1536,2048]{1,0:T(8,128)(2,1)} fusion(bf16[2304,2048]{1,0:T(8,128)(2,1)} %reshape.75, s32[2048]{0:T(1024)S(1)} %pad_clamp_fusion.1), kind=kCustom, calls=%fused_computation.1 | custom fusion | bytes 12589056 | tf_op jit(solution)/shard_map/gather | solution.py:50
  651.1 11.9 %reshape.76 = f32[384,4,2048]{2,1,0:T(4,128)} reshape(bf16[1536,2048]{1,0:T(8,128)(2,1)} %gather_fusion.1) | data formatting | bytes 18874368 | tf_op jit(solution)/shard_map/convert_element_type | solution.py:50
  662.9 11.9 %reduce_sum.32 = f32[384,2048]{1,0:T(8,128)} reduce(f32[384,4,2048]{2,1,0:T(4,128)} %reshape.76, f32[]{:T(128)} %constant.42.clone.1), dimensions={1}, to_apply=%region_7.8 | reduce | flops 2359296 | bytes 15728644 | tf_op jit(solution)/shard_map/reduce_sum | solution.py:51
  674.8 3.4 add_convert_fusion
  (23 shorter events, 0.7 us)
Async XLA Ops:
  6.5 373.2 %copy-start = (bf16[512,2048]{1,0:T(8,128)(2,1)S(1)}, bf16[512,2048]{1,0:T(8,128)(2,1)}, u32[]{:S(2)}) copy-start(bf16[512,2048]{1,0:T(8,128)(2,1)} %param.12) | copy-start | bytes 6291460
  8.8 1.4 copy-start.2
  12.0 10.7 %copy-start.3 = (f32[2048]{0:T(1024)S(1)}, f32[2048]{0:T(1024)}, u32[]{:S(2)}) copy-start(f32[2048]{0:T(1024)} %param.13) | copy-start | bytes 24580
  100.1 217.3 %all-to-all-start = ((bf16[64,4,9,2048]{3,1,2,0:T(4,128)(2,1)}), bf16[64,4,9,2048]{3,1,2,0:T(4,128)(2,1)}, u32[]{:S(2)}, u32[]{:S(2)}) async-start(bf16[64,4,9,2048]{3,1,2,0:T(4,128)(2,1)} %copy.33), calls=%async_computation | async-start | bytes 18874368 | tf_op jit(solution)/shard_map/all_to_all | solution.py:34
  112.3 267.4 %all-reduce.2.cloned.1.call-start = ((), (), s32[]{:S(2)}) async-start(), calls=%async_computation.2 | async-start | bytes 2359296 | tf_op jit(solution)/shard_map/psum | solution.py:38
  317.3 62.4 %copy-start.4 = (f32[512]{0:T(512)S(1)}, f32[512]{0:T(512)}, u32[]{:S(2)}) copy-start(f32[512]{0:T(512)} %param.11) | copy-start | bytes 6148
  391.2 215.8 %all-to-all-start.1 = ((bf16[64,4,9,2048]{3,1,2,0:T(4,128)(2,1)}), bf16[64,4,9,2048]{3,1,2,0:T(4,128)(2,1)}, u32[]{:S(2)}, u32[]{:S(2)}) async-start(bf16[64,4,9,2048]{3,1,2,0:T(4,128)(2,1)} %copy.36), calls=%async_computation.1 | async-start | bytes 18874368 | tf_op jit(solution)/shard_map/all_to_all | solution.py:40
  662.9 15.3 %copy-start.1 = (bf16[512,2048]{1,0:T(8,128)(2,1)S(1)}, bf16[512,2048]{1,0:T(8,128)(2,1)}, u32[]{:S(2)}) copy-start(bf16[512,2048]{1,0:T(8,128)(2,1)} %param.12) | copy-start | bytes 6291460
Sparse Core Ops, SparseCore 0:
  328.0 51.7 all-reduce.1
where the time goes:
time: 691 us; the launch traced here: 685 us
  waiting for transfers between devices  458 us (66%)
  local copies, waits for them, and re-layouts  144 us (21%)
  other arithmetic  32 us (5%)
  starting transfers between devices  23.3 us (3%)
  matrix products  14.6 us (2%)
  between operations  13.6 us (2%)
    all_to_all x1, waiting for transfers between devices, local(): lax.all_to_all(jnp.einsum('sbch,bhd->sbcd', codes, dec_blocks, preferred_...  205 us
    all_to_all x1, waiting for transfers between devices, local(): lax.all_to_all(outgoing, ('seq', 'lat'), split_axis=0, concat_axis=0, til...  201 us
    psum x1, waiting for transfers between devices, local(): summed = lax.psum(preact, 'tp')  51.9 us
    gather x2, local copies, waits for them, and re-layouts, local(): centered[slot_row]  35 us
    select_n x1, local copies, waits for them, and re-layouts, local(): jnp.where(filled[:, None], centered[slot_row], jnp.zeros((), jnp.bfloat16))  19.6 us
    gather x1, local copies, waits for them, and re-layouts, local(): contrib = returned[target].reshape(rows, top, width).astype(jnp.float32)  17.6 us
    reshape x1, local copies, waits for them, and re-layouts, local(): returned = returned.reshape(nblocks * capacity, width)  15.8 us
  transfers between devices with their start and end apart: 3, of which 3 were waited for; matrix products, arithmetic and copies ran while one was open for 1% of the time, Pallas kernels for 0%

commit v1 on v0

v1 whole, which is shorter than its diff:
```python
import jax
import jax.numpy as jnp
from jax import lax
from jax.experimental import pallas as pl
from jax.experimental.pallas import tpu as pltpu
from jax.sharding import PartitionSpec as P

NX, NZ = 4, 8
PAD = 16
MESH = pl.DeviceIdType.MESH
BF, F32 = jnp.bfloat16, jnp.float32


def kernel(tokens, act, table, enc, bias, dec, dbias, out, tokbuf,
           enc_all, dec_all, bias_all, tgt, stage, last, work, picks, preact, parts_in, codes,
           rs_first, rs_in,
           tok_s, tok_r, tgt_s, tgt_r, w_s, w_r, ys_s, ys_r, yc_s, yc_r, rs_s, rs_r, loc):
    rows, width = tokens.shape
    half = rows // 2
    blocks = table.shape[0]
    row_blocks = blocks // NZ
    slots = row_blocks * PAD
    quarter = slots // 4
    s, y, c = lax.axis_index("seq"), lax.axis_index("tp"), lax.axis_index("lat")
    x, z = s // NZ, s % NZ

    def at(dx=0, dz=0, dy=0, dc=0):
        return (((x + dx + NX) % NX) * NZ + (z + dz + NZ) % NZ, (y + dy) % 4, (c + dc) % 2)

    def member(dx=0, dc=0):
        return ((x + dx + NX) % NX) * 2 + (c + dc) % 2

    def send(src, dst, ss, rs, dev):
        copy = pltpu.make_async_remote_copy(src_ref=src, dst_ref=dst, send_sem=ss, recv_sem=rs,
                                            device_id=dev, device_id_type=MESH)
        copy.start()
        return copy

    sent = []
    peers = [at(dz=1), at(dz=-1), at(dx=1), at(dx=-1), at(dc=1), at(dy=1), at(dy=2), at(dy=3)]
    barrier = pltpu.get_barrier_semaphore()
    for dev in peers:
        pl.semaphore_signal(barrier, inc=1, device_id=dev, device_id_type=MESH)
    pl.semaphore_wait(barrier, len(peers))

    def part(ref, h):
        return ref.at[pl.ds(h * half, half)]

    tok = {}

    def tok_send(d, k, o):
        h = o if d == 0 else 1 - o
        src = tokens if k == 0 else tokbuf.at[2 * k - 2 + d]
        dst = last if k == 3 else tokbuf.at[2 * k + d]
        tok[d, k, o] = send(part(src, h), part(dst, h), tok_s.at[d, k, o], tok_r.at[d, k, o],
                            at(dz=1 if d == 0 else -1))
        sent.append(tok[d, k, o])

    tg = {}

    def tgt_send(d, k):
        src = 0 if k == 0 else 2 * k - 1 + d
        dst = 7 if k == 3 else 2 * k + 1 + d
        tg[d, k] = send(tgt.at[src], tgt.at[dst], tgt_s.at[d, k], tgt_r.at[d, k], at(dz=1 if d == 0 else -1))
        sent.append(tg[d, k])

    wc = {}
    store = (enc_all, dec_all, bias_all)
    own = (enc, dec, bias)

    def w_send(kind, slot, m, dev, first=False, piece=None):
        dst = store[kind].at[m]
        src = own[kind] if first else dst
        if piece is not None:
            n = src.shape[0] // 2
            src, dst = src.at[pl.ds(piece * n, n)], dst.at[pl.ds(piece * n, n)]
        wc[kind, slot] = send(src, dst, w_s.at[kind, slot], w_r.at[kind, slot], dev)
        sent.append(wc[kind, slot])

    def w_start(kind):
        w_send(kind, 0, member(), at(dx=1), first=True)
        w_send(kind, 1, member(), at(dx=-1), first=True)
        w_send(kind, 2, member(), at(dc=1), first=True)

    def w_second(kind):
        wc[kind, 0].wait_recv()
        if kind == 2:
            w_send(kind, 3, member(-1), at(dx=1))
        else:
            w_send(kind, 3, member(-1), at(dx=1), piece=0)
        wc[kind, 1].wait_recv()
        if kind != 2:
            w_send(kind, 4, member(1), at(dx=-1), piece=1)
        w_send(kind, 5, member(-1), at(dc=1))
        w_send(kind, 6, member(1), at(dc=1))

    def w_third(kind):
        wc[kind, 3].wait_recv()
        if kind != 2:
            wc[kind, 4].wait_recv()
        w_send(kind, 7, member(2), at(dc=1))

    def w_done(kind):
        for slot in (2, 5, 6, 7):
            wc[kind, slot].wait_recv()

    tok_send(0, 0, 0)
    tok_send(1, 0, 0)
    tok_send(0, 0, 1)
    tok_send(1, 0, 1)
    w_start(2)
    w_start(0)
    local = [pltpu.make_async_copy(tokens, stage, loc.at[0]),
             pltpu.make_async_copy(enc, enc_all.at[member()], loc.at[1]),
             pltpu.make_async_copy(dec, dec_all.at[member()], loc.at[2]),
             pltpu.make_async_copy(bias, bias_all.at[member()], loc.at[3])]
    for copy in local:
        copy.start()

    ids = lax.broadcasted_iota(jnp.int32, (blocks, rows), 0)
    hits = [act[pl.ds(k, 1), :] == ids for k in range(4)]
    named = (hits[0] | hits[1]) | (hits[2] | hits[3])
    before = (lax.broadcasted_iota(jnp.int32, (rows, rows), 0)
              < lax.broadcasted_iota(jnp.int32, (rows, rows), 1))
    rank = jnp.dot(jnp.where(named, 1.0, 0.0).astype(BF), jnp.where(before, 1.0, 0.0).astype(BF),
                   preferred_element_type=F32)
    where_to = rank + table[...]
    for k in range(4):
        tgt[0, pl.ds(k, 1), :] = jnp.sum(jnp.where(hits[k], where_to, 0.0), axis=0, keepdims=True)
    tgt[0, pl.ds(4, 4), :] = jnp.full((4, rows), -1.0, F32)
    tgt_send(0, 0)
    tgt_send(1, 0)

    base = (z * slots).astype(F32)

    def encode(ref, i):
        def pick(j, carry):
            n = slots // 4
            r0 = pl.multiple_of(j * n, n)
            place = (lax.broadcasted_iota(jnp.int32, (n, rows), 0) + r0).astype(F32) + base
            t = tgt[i]
            hit = ((t[0:1] == place) | (t[1:2] == place)) | ((t[2:3] == place) | (t[3:4] == place))
            picks[pl.ds(r0, n), :] = jnp.where(hit, 1.0, 0.0).astype(BF)
            return carry

        lax.fori_loop(0, 4, pick, 0)

        def gather(j, carry):
            n = width // 4
            c0 = pl.multiple_of(j * n, n)
            got = jnp.dot(picks[...], ref[:, pl.ds(c0, n)], preferred_element_type=F32)
            work[0, :, pl.ds(c0, n)] = (got - dbias[:, pl.ds(c0, n)]).astype(BF)
            return carry

        lax.fori_loop(0, 4, gather, 0)

        def one(m, carry):
            for b in range(4):
                r0 = pl.multiple_of((m * 4 + b) * PAD, PAD)
                preact[i, pl.ds(r0, PAD), :] = jnp.dot(
                    work[0, pl.ds(r0, PAD), :], enc_all[m, :, pl.ds(b * 128, 128)], preferred_element_type=F32)
            return carry

        lax.fori_loop(0, 8, one, 0)

    ysum, ycode = {}, {}

    def y_start(g, i, n):
        for o in range(1, 4):
            to = pl.multiple_of(((y + o) % 4) * quarter, quarter)
            ysum[g, o] = send(preact.at[pl.ds(i, n), pl.ds(to, quarter)], parts_in.at[o - 1, pl.ds(i, n)],
                              ys_s.at[g, o - 1], ys_r.at[g, o - 1], at(dy=o))
            sent.append(ysum[g, o])

    mine = pl.multiple_of(y * quarter, quarter)

    def y_codes(g, i, n):
        for o in range(1, 4):
            ysum[g, o].wait_recv()
        per = bias_all[pl.ds(2 * y, 2)].reshape(quarter // PAD, 1, 128)
        for j in range(i, i + n):
            total = preact[j, pl.ds(mine, quarter), :] + parts_in[0, j] + parts_in[1, j] + parts_in[2, j]
            total = total.reshape(quarter // PAD, PAD, 128) + per
            codes[j, pl.ds(mine, quarter), :] = jnp.maximum(total, 0.0).astype(BF).reshape(quarter, 128)
        for o in range(1, 4):
            view = codes.at[pl.ds(i, n), pl.ds(mine, quarter)]
            ycode[g, o] = send(view, view, yc_s.at[g, o - 1], yc_r.at[g, o - 1], at(dy=o))
            sent.append(ycode[g, o])

    def y_done(g):
        for o in range(1, 4):
            ycode[g, o].wait_recv()

    def tok_pass(k, o):
        for d in range(2):
            tok[d, k, o].wait_recv()
            if k < 2 or o == 0:
                tok_send(d, k + 1, o)

    def tgt_pass(k):
        for d in range(2):
            tg[d, k].wait_recv()
            if k < 2 or d == 0:
                tgt_send(d, k + 1)

    def staged(g):
        def step(j, carry):
            i = 2 * g - 1 + j
            copy = pltpu.make_async_copy(tokbuf.at[i - 1], stage, loc.at[4])
            copy.start()
            copy.wait()
            encode(stage, i)
            return carry

        lax.fori_loop(0, 2, step, 0)
        y_start(g, 2 * g - 1, 2)

    tgt_pass(0)
    tok_pass(0, 0)
    w_second(2)
    w_third(2)
    tok_pass(0, 1)
    tgt_pass(1)
    w_second(0)
    w_start(1)
    tok_pass(1, 0)
    tgt_pass(2)
    for copy in local:
        copy.wait()
    tok_pass(1, 1)
    w_third(0)
    w_done(2)
    w_done(0)
    encode(stage, 0)
    y_start(0, 0, 1)
    staged(1)
    y_codes(0, 0, 1)
    tok_pass(2, 0)
    staged(2)
    y_codes(1, 1, 2)
    w_second(1)
    tok_pass(2, 1)
    staged(3)
    y_codes(2, 3, 2)
    tg[0, 3].wait_recv()
    tok[0, 3, 0].wait_recv()
    tok[1, 3, 0].wait_recv()
    encode(last, 7)
    y_start(4, 7, 1)
    y_codes(3, 5, 2)
    w_third(1)
    y_codes(4, 7, 1)
    w_done(1)
    for g in range(5):
        y_done(g)

    def decode(i, buf):
        def one(m, carry):
            for b in range(4):
                r0 = pl.multiple_of((m * 4 + b) * PAD, PAD)
                work[buf, pl.ds(r0, PAD), :] = jnp.dot(
                    codes[i, pl.ds(r0, PAD), :], dec_all[m, pl.ds(b * 128, 128), :],
                    preferred_element_type=F32).astype(BF)
            return carry

        lax.fori_loop(0, 8, one, 0)

    def spread(i, h):
        t = jnp.concatenate([tgt[i], jnp.zeros((120, rows), F32)], axis=0)
        cols = jnp.transpose(t)[h * half:(h + 1) * half]
        place = lax.broadcasted_iota(jnp.int32, (half, slots), 1).astype(F32) + base
        hit = (((cols[:, 0:1] == place) | (cols[:, 1:2] == place))
               | ((cols[:, 2:3] == place) | (cols[:, 3:4] == place)))
        return jnp.where(hit, 1.0, 0.0).astype(BF)

    def combine(i, buf, h, dst, plus=()):
        sel = spread(i, h)
        for j in range(4):
            n = width // 4
            cs = pl.ds(j * n, n)
            total = jnp.dot(sel, work[buf, :, cs], preferred_element_type=F32)
            for ref in plus:
                total = total + ref[:, cs].astype(F32)
            dst[:, cs] = total.astype(BF)

    rs = {}

    def rs_send(d, k, o, src):
        rs[d, k, o] = send(src, rs_in.at[d, k, o], rs_s.at[d, k, o], rs_r.at[d, k, o],
                           at(dz=1 if d == 0 else -1))
        sent.append(rs[d, k, o])

    decode(7, 0)
    for d in range(2):
        combine(7, 0, d, rs_first.at[d, 0])
        rs_send(d, 0, 0, rs_first.at[d, 0])
    for k in range(1, 4):
        idx = (8 - 2 * k, 7 - 2 * k)
        for d in range(2):
            decode(idx[d], d)
        if k == 1:
            for d in range(2):
                combine(idx[d], d, 1 - d, rs_first.at[d, 1])
                rs_send(d, 1, 1, rs_first.at[d, 1])
        for o in range(2):
            if k == 1 and o == 1:
                continue
            for d in range(2):
                got = rs_in.at[d, k - 1, o]
                rs[d, k - 1, o].wait_recv()
                combine(idx[d], d, o if d == 0 else 1 - o, got, (got,))
                rs_send(d, k, o, got)
    decode(0, 0)
    for o in range(2):
        rs[0, 3, o].wait_recv()
        rs[1, 3, 1 - o].wait_recv()
        combine(0, 0, o, out.at[pl.ds(o * half, half)], (rs_in.at[0, 3, o], rs_in.at[1, 3, 1 - o], dbias))
    for copy in sent:
        copy.wait_send()


def local(tokens, active, placement_map, enc_weight, enc_bias, dec_weight, dec_bias):
    rows, width = tokens.shape
    blocks = placement_map.shape[0]
    slots = blocks // NZ * PAD
    depth = enc_weight.shape[1]
    p = placement_map
    table = ((p // 8) % NZ * slots + (p // (8 * NZ) * 8 + p % 8) * PAD).astype(F32).reshape(blocks, 1)
    vmem, hbm = pl.BlockSpec(memory_space=pltpu.VMEM), pl.BlockSpec(memory_space=pl.ANY)
    half = rows // 2
    dma = pltpu.SemaphoreType.DMA
    out, _ = pl.pallas_call(
        kernel,
        out_shape=(jax.ShapeDtypeStruct((rows, width), BF), jax.ShapeDtypeStruct((6, rows, width), BF)),
        in_specs=[hbm, vmem, vmem, hbm, vmem, hbm, vmem],
        out_specs=(vmem, hbm),
        scratch_shapes=[
            pltpu.VMEM((8, width, depth), BF),
            pltpu.VMEM((8, depth, width), BF),
            pltpu.VMEM((8, 4, 128), F32),
            pltpu.VMEM((8, 8, rows), F32),
            pltpu.VMEM((rows, width), BF),
            pltpu.VMEM((rows, width), BF),
            pltpu.VMEM((2, slots, width), BF),
            pltpu.VMEM((slots, rows), BF),
            pltpu.VMEM((8, slots, 128), F32),
            pltpu.VMEM((3, 8, slots // 4, 128), F32),
            pltpu.VMEM((8, slots, 128), BF),
            pltpu.VMEM((2, 2, half, width), BF),
            pltpu.VMEM((2, 4, 2, half, width), BF),
            dma((2, 4, 2)), dma((2, 4, 2)),
            dma((2, 4)), dma((2, 4)),
            dma((3, 8)), dma((3, 8)),
            dma((5, 3)), dma((5, 3)),
            dma((5, 3)), dma((5, 3)),
            dma((2, 4, 2)), dma((2, 4, 2)),
            dma((5,)),
        ],
        compiler_params=pltpu.CompilerParams(collective_id=0, has_side_effects=True, vmem_limit_bytes=63 << 20),
        name="encode_decode",
    )(tokens, active.T, table, enc_weight, enc_bias.reshape(4, 128), dec_weight, dec_bias.reshape(1, width))
    return out


def solution(mesh):
    return jax.shard_map(
        local,
        mesh=mesh,
        in_specs=(
            P(("seq", "lat"), "tp"),
            P(("seq", "lat"), None),
            P(),
            P("tp", ("seq", "lat")),
            P(("seq", "lat")),
            P(("seq", "lat"), "tp"),
            P("tp"),
        ),
        out_specs=P(("seq", "lat"), "tp"),
        check_vma=False,
    )
```

time: 691 us -> 286 us (0.41)
  waiting for transfers between devices: 458 us -> 0 us
  Pallas kernels: 0 us -> 281 us
  local copies, waits for them, and re-layouts: 144 us -> 3.53 us
  other arithmetic: 32 us -> 0.7 us
  starting transfers between devices: 23.3 us -> 0 us
  matrix products: 14.6 us -> 0 us
  between operations: 13.6 us -> 0.01 us
    all_to_all x2 -> x0, waiting for transfers between devices: 406 us -> none  [the longest x1 205 us: local(): lax.all_to_all(jnp.einsum('sbch,bhd->sbcd', codes, dec_blocks, preferred_...]
    pallas_call x0 -> x1, Pallas kernels: none -> 281 us  [local(): pl.pallas_call(kernel, out_shape=(jax.ShapeDtypeStruct((rows, width), BF)...]
    gather x3 -> x0, local copies, waits for them, and re-layouts: 52.6 us -> none  [the longest x2 35 us: local(): centered[slot_row]]
    psum x1 -> x0, waiting for transfers between devices: 51.9 us -> none  [local(): summed = lax.psum(preact, 'tp')]
    all_to_all x2 -> x0, starting transfers between devices: 23.1 us -> none  [the longest x1 12.3 us: local(): lax.all_to_all(outgoing, ('seq', 'lat'), split_axis=0, concat_axis=0, til...]
    select_n x1 -> x0, local copies, waits for them, and re-layouts: 19.6 us -> none  [local(): jnp.where(filled[:, None], centered[slot_row], jnp.zeros((), jnp.bfloat16))]
    convert_element_type x2 -> x0, local copies, waits for them, and re-layouts: 19.2 us -> none  [the longest x1 11.9 us: local(): contrib = returned[target].reshape(rows, top, width).astype(jnp.float32)]
    reshape x2 -> x1, local copies, waits for them, and re-layouts: 19.8 us -> 0.8 us  [local(): (p // 8 % NZ * slots + (p // (8 * NZ) * 8 + p % 8) * PAD).astype(F32)]
  transfers between devices with their start and end apart: 3 -> 0, of which waited for: 3 -> 0; matrix products, arithmetic and copies ran while one was open for 1% -> 0% of each run, Pallas kernels for 0% -> 0%
where the time goes in v1:
time: 286 us; the launch traced here: 285 us
  Pallas kernels  281 us (98%)
  local copies, waits for them, and re-layouts  3.53 us (1%)
    pallas_call x1, Pallas kernels, local(): pl.pallas_call(kernel, out_shape=(jax.ShapeDtypeStruct((rows, width), BF)...  281 us

profile of v1, /device:TPU:4, one launch (start us, length us, event | category | flops | bytes accessed | tf_op | source)
XLA Modules:
  0.0 284.9 jit_solution(8843883618175618788)
XLA Ops:
  0.0 0.7 fusion.4
  0.7 0.8 copy.8.table
  1.5 280.7 %encode_decode.1 = (bf16[384,2048]{1,0:T(8,128)(2,1)}, bf16[6,384,2048]{2,1,0:T(8,128)(2,1)}) custom-call(bf16[384,2048]{1,0:T(8,128)(2,1)} %tokens.1, s32[4,384]{1,0:T(4,128)} %bitcast.5, f32[256,1]{1,0:T(8,128)} %copy.8.table, bf16[2048,512]{1,0:T(8,128)(2,1)} %enc.1, f32[4,128]{1,0:T(4,128)} %bitcast.7, bf16[512,2048]{1,0:T(8,128)(2,1)} %dec.1, ...), custom_call_target="tpu_custom_call" | custom-call | tf_op jit(solution)/shard_map/encode_decode/pallas_call | solution.py:332
  282.2 2.7 copy.10

commit v2 on v1

--- a/solution.py
+++ b/solution.py
@@ -12,7 +12,7 @@
 
 
 def kernel(tokens, act, table, enc, bias, dec, dbias, out, tokbuf,
-           enc_all, dec_all, bias_all, tgt, stage, last, work, picks, preact, parts_in, codes,
+           enc_all, dec_all, bias_all, tgt, stage, last, work, picks, preact, parts_in, codes, sels,
            rs_first, rs_in,
            tok_s, tok_r, tgt_s, tgt_r, w_s, w_r, ys_s, ys_r, yc_s, yc_r, rs_s, rs_r, loc):
     rows, width = tokens.shape
@@ -77,39 +77,55 @@
         wc[kind, slot] = send(src, dst, w_s.at[kind, slot], w_r.at[kind, slot], dev)
         sent.append(wc[kind, slot])
 
-    def w_start(kind):
-        w_send(kind, 0, member(), at(dx=1), first=True)
-        w_send(kind, 1, member(), at(dx=-1), first=True)
-        w_send(kind, 2, member(), at(dc=1), first=True)
-
-    def w_second(kind):
+    def w_first(kind):
+        for p in range(2):
+            w_send(kind, p, member(), at(dx=1), first=True, piece=p)
+            w_send(kind, 3 - p, member(), at(dx=-1), first=True, piece=1 - p)
+        w_send(kind, 6, member(), at(dc=1), first=True)
+
+    def w_pass(kind):
         wc[kind, 0].wait_recv()
-        if kind == 2:
-            w_send(kind, 3, member(-1), at(dx=1))
-        else:
-            w_send(kind, 3, member(-1), at(dx=1), piece=0)
+        w_send(kind, 4, member(-1), at(dx=1), piece=0)
+        wc[kind, 3].wait_recv()
+        w_send(kind, 5, member(1), at(dx=-1), piece=1)
+
+    def w_mid(kind):
         wc[kind, 1].wait_recv()
-        if kind != 2:
-            w_send(kind, 4, member(1), at(dx=-1), piece=1)
-        w_send(kind, 5, member(-1), at(dc=1))
-        w_send(kind, 6, member(1), at(dc=1))
-
-    def w_third(kind):
-        wc[kind, 3].wait_recv()
-        if kind != 2:
-            wc[kind, 4].wait_recv()
-        w_send(kind, 7, member(2), at(dc=1))
-
-    def w_done(kind):
-        for slot in (2, 5, 6, 7):
+        w_send(kind, 7, member(-1), at(dc=1))
+        wc[kind, 2].wait_recv()
+        w_send(kind, 8, member(1), at(dc=1))
+
+    def w_last(kind):
+        for p in range(2):
+            wc[kind, 4 + p].wait_recv()
+            w_send(kind, 9 + p, member(2), at(dc=1), piece=p)
+
+    def w_done(kind, slots):
+        for slot in slots:
             wc[kind, slot].wait_recv()
+
+    def b_first():
+        w_send(2, 0, member(), at(dx=1), first=True)
+        w_send(2, 1, member(), at(dx=-1), first=True)
+        w_send(2, 6, member(), at(dc=1), first=True)
+
+    def b_pass():
+        wc[2, 0].wait_recv()
+        w_send(2, 4, member(-1), at(dx=1))
+        w_send(2, 7, member(-1), at(dc=1))
+        wc[2, 1].wait_recv()
+        w_send(2, 8, member(1), at(dc=1))
+
+    def b_last():
+        wc[2, 4].wait_recv()
+        w_send(2, 9, member(2), at(dc=1))
 
     tok_send(0, 0, 0)
     tok_send(1, 0, 0)
     tok_send(0, 0, 1)
     tok_send(1, 0, 1)
-    w_start(2)
-    w_start(0)
+    b_first()
+    w_first(0)
     local = [pltpu.make_async_copy(tokens, stage, loc.at[0]),
              pltpu.make_async_copy(enc, enc_all.at[member()], loc.at[1]),
              pltpu.make_async_copy(dec, dec_all.at[member()], loc.at[2]),
@@ -215,47 +231,10 @@
         lax.fori_loop(0, 2, step, 0)
         y_start(g, 2 * g - 1, 2)
 
-    tgt_pass(0)
-    tok_pass(0, 0)
-    w_second(2)
-    w_third(2)
-    tok_pass(0, 1)
-    tgt_pass(1)
-    w_second(0)
-    w_start(1)
-    tok_pass(1, 0)
-    tgt_pass(2)
-    for copy in local:
-        copy.wait()
-    tok_pass(1, 1)
-    w_third(0)
-    w_done(2)
-    w_done(0)
-    encode(stage, 0)
-    y_start(0, 0, 1)
-    staged(1)
-    y_codes(0, 0, 1)
-    tok_pass(2, 0)
-    staged(2)
-    y_codes(1, 1, 2)
-    w_second(1)
-    tok_pass(2, 1)
-    staged(3)
-    y_codes(2, 3, 2)
-    tg[0, 3].wait_recv()
-    tok[0, 3, 0].wait_recv()
-    tok[1, 3, 0].wait_recv()
-    encode(last, 7)
-    y_start(4, 7, 1)
-    y_codes(3, 5, 2)
-    w_third(1)
-    y_codes(4, 7, 1)
-    w_done(1)
-    for g in range(5):
-        y_done(g)
-
-    def decode(i, buf):
-        def one(m, carry):
+    def decode(i, buf, lo=0, hi=8):
+        def one(j, carry):
+            q = j // 2
+            m = ((x + q + q // 2 - 2 * (q // 3)) % NX) * 2 + j % 2
             for b in range(4):
                 r0 = pl.multiple_of((m * 4 + b) * PAD, PAD)
                 work[buf, pl.ds(r0, PAD), :] = jnp.dot(
@@ -263,7 +242,7 @@
                     preferred_element_type=F32).astype(BF)
             return carry
 
-        lax.fori_loop(0, 8, one, 0)
+        lax.fori_loop(lo, hi, one, 0)
 
     def spread(i, h):
         t = jnp.concatenate([tgt[i], jnp.zeros((120, rows), F32)], axis=0)
@@ -273,14 +252,17 @@
                | ((cols[:, 2:3] == place) | (cols[:, 3:4] == place)))
         return jnp.where(hit, 1.0, 0.0).astype(BF)
 
-    def combine(i, buf, h, dst, plus=()):
-        sel = spread(i, h)
+    def sums(h, buf, plus):
         for j in range(4):
             n = width // 4
             cs = pl.ds(j * n, n)
-            total = jnp.dot(sel, work[buf, :, cs], preferred_element_type=F32)
+            total = jnp.dot(sels[h], work[buf, :, cs], preferred_element_type=F32)
             for ref in plus:
                 total = total + ref[:, cs].astype(F32)
+            yield cs, total
+
+    def combine(h, buf, dst, plus=()):
+        for cs, total in sums(h, buf, plus):
             dst[:, cs] = total.astype(BF)
 
     rs = {}
@@ -288,33 +270,97 @@
     def rs_send(d, k, o, src):
         rs[d, k, o] = send(src, rs_in.at[d, k, o], rs_s.at[d, k, o], rs_r.at[d, k, o],
                            at(dz=1 if d == 0 else -1))
-        sent.append(rs[d, k, o])
-
-    decode(7, 0)
-    for d in range(2):
-        combine(7, 0, d, rs_first.at[d, 0])
-        rs_send(d, 0, 0, rs_first.at[d, 0])
-    for k in range(1, 4):
-        idx = (8 - 2 * k, 7 - 2 * k)
-        for d in range(2):
-            decode(idx[d], d)
-        if k == 1:
+        if k > 1 or (k == 1 and o == 0):
+            sent.append(rs[d, k, o])
+
+    def rs_phase():
+        for d in range(2):
+            combine(d, 0, rs_first.at[d, 0])
+            rs_send(d, 0, 0, rs_first.at[d, 0])
+        for k in range(1, 4):
+            idx = (8 - 2 * k, 7 - 2 * k)
             for d in range(2):
-                combine(idx[d], d, 1 - d, rs_first.at[d, 1])
-                rs_send(d, 1, 1, rs_first.at[d, 1])
-        for o in range(2):
-            if k == 1 and o == 1:
-                continue
-            for d in range(2):
-                got = rs_in.at[d, k - 1, o]
-                rs[d, k - 1, o].wait_recv()
-                combine(idx[d], d, o if d == 0 else 1 - o, got, (got,))
-                rs_send(d, k, o, got)
-    decode(0, 0)
-    for o in range(2):
-        rs[0, 3, o].wait_recv()
-        rs[1, 3, 1 - o].wait_recv()
-        combine(0, 0, o, out.at[pl.ds(o * half, half)], (rs_in.at[0, 3, o], rs_in.at[1, 3, 1 - o], dbias))
+                decode(idx[d], d)
+            if k == 1:
+                for d in range(2):
+                    sels[1 - d] = spread(idx[d], 1 - d)
+                    combine(1 - d, d, rs_first.at[d, 1])
+                    rs_send(d, 1, 1, rs_first.at[d, 1])
+            for o in range(2):
+                if k == 1 and o == 1:
+                    continue
+                for d in range(2):
+                    got = rs_in.at[d, k - 1, o]
+                    h = o if d == 0 else 1 - o
+                    sels[h] = spread(idx[d], h)
+                    rs[d, k - 1, o].wait_recv()
+                    combine(h, d, got, (got,))
+                    rs_send(d, k, o, got)
+        decode(0, 0)
+        for d in range(2):
+            rs[d, 0, 0].wait_send()
+            rs[d, 1, 1].wait_send()
+            sels[d] = spread(0, d)
+        for d in range(2):
+            rs[d, 3, 0].wait_recv()
+            for cs, total in sums(d, 0, (rs_in.at[d, 3, 0], dbias)):
+                top = total.astype(BF)
+                rs_first[0, d, :, cs] = top
+                rs_first[1, d, :, cs] = (total - top.astype(F32)).astype(BF)
+        for d in range(2):
+            h = 1 - d
+            rs[d, 3, 1].wait_recv()
+            for j in range(4):
+                cs = pl.ds(j * (width // 4), width // 4)
+                total = rs_first[0, h, :, cs].astype(F32) + rs_first[1, h, :, cs].astype(F32)
+                out[pl.ds(h * half, half), cs] = (total + rs_in[d, 3, 1, :, cs].astype(F32)).astype(BF)
+
+    b_pass()
+    tok_pass(0, 0)
+    w_pass(0)
+    w_first(1)
+    tok_pass(0, 1)
+    tgt_pass(0)
+    w_mid(0)
+    b_last()
+    tok_pass(1, 0)
+    for copy in local:
+        copy.wait()
+    tok_pass(1, 1)
+    tgt_pass(1)
+    w_last(0)
+    w_done(2, (6, 7, 8, 9))
+    w_done(0, (6, 7, 8, 9, 10))
+    encode(stage, 0)
+    y_start(0, 0, 1)
+    staged(1)
+    tok_pass(2, 0)
+    y_codes(0, 0, 1)
+    w_pass(1)
+    staged(2)
+    y_codes(1, 1, 2)
+    tok_pass(2, 1)
+    tgt_pass(2)
+    staged(3)
+    y_codes(2, 3, 2)
+    w_mid(1)
+    tok[0, 3, 0].wait_recv()
+    tok[1, 3, 0].wait_recv()
+    tg[0, 3].wait_recv()
+    encode(last, 7)
+    y_start(4, 7, 1)
+    y_codes(3, 5, 2)
+    for h in range(2):
+        sels[h] = spread(7, h)
+    y_codes(4, 7, 1)
+    for g in range(5):
+        y_done(g)
+    w_done(1, (6, 7, 8))
+    decode(7, 0, 0, 6)
+    w_last(1)
+    w_done(1, (9, 10))
+    decode(7, 0, 6, 8)
+    rs_phase()
     for copy in sent:
         copy.wait_send()
 
@@ -346,11 +392,12 @@
             pltpu.VMEM((8, slots, 128), F32),
             pltpu.VMEM((3, 8, slots // 4, 128), F32),
             pltpu.VMEM((8, slots, 128), BF),
+            pltpu.VMEM((2, half, slots), BF),
             pltpu.VMEM((2, 2, half, width), BF),
             pltpu.VMEM((2, 4, 2, half, width), BF),
             dma((2, 4, 2)), dma((2, 4, 2)),
             dma((2, 4)), dma((2, 4)),
-            dma((3, 8)), dma((3, 8)),
+            dma((3, 11)), dma((3, 11)),
             dma((5, 3)), dma((5, 3)),
             dma((5, 3)), dma((5, 3)),
             dma((2, 4, 2)), dma((2, 4, 2)),

time: 286 us -> 287 us (level)
  no operation moved by 1% of the time
where the time goes in v2:
time: 287 us; the launch traced here: 285 us
  Pallas kernels  281 us (98%)
  local copies, waits for them, and re-layouts  3.53 us (1%)
    pallas_call x1, Pallas kernels, local(): pl.pallas_call(kernel, out_shape=(jax.ShapeDtypeStruct((rows, width), BF)...  281 us

profile of v2, /device:TPU:4, one launch (start us, length us, event | category | flops | bytes accessed | tf_op | source)
XLA Modules:
  0.0 285.0 jit_solution(17828109204182225935)
XLA Ops:
  0.0 0.7 fusion.4
  0.7 0.8 copy.8.table
  1.5 280.8 %encode_decode.1 = (bf16[384,2048]{1,0:T(8,128)(2,1)}, bf16[6,384,2048]{2,1,0:T(8,128)(2,1)}) custom-call(bf16[384,2048]{1,0:T(8,128)(2,1)} %tokens.1, s32[4,384]{1,0:T(4,128)} %bitcast.5, f32[256,1]{1,0:T(8,128)} %copy.8.table, bf16[2048,512]{1,0:T(8,128)(2,1)} %enc.1, f32[4,128]{1,0:T(4,128)} %bitcast.7, bf16[512,2048]{1,0:T(8,128)(2,1)} %dec.1, ...), custom_call_target="tpu_custom_call" | custom-call | tf_op jit(solution)/shard_map/encode_decode/pallas_call | solution.py:378
  282.3 2.7 copy.10

commit v3 on v2

--- a/solution.py
+++ b/solution.py
@@ -65,15 +65,20 @@
         sent.append(tg[d, k])
 
     wc = {}
-    store = (enc_all, dec_all, bias_all)
-    own = (enc, dec, bias)
+    store = (enc_all, dec_all, dec_all, bias_all)
+    own = (enc, dec, dec, bias)
+    side = width // 2
 
     def w_send(kind, slot, m, dev, first=False, piece=None):
         dst = store[kind].at[m]
         src = own[kind] if first else dst
-        if piece is not None:
-            n = src.shape[0] // 2
-            src, dst = src.at[pl.ds(piece * n, n)], dst.at[pl.ds(piece * n, n)]
+        n = src.shape[0] if piece is None else src.shape[0] // 2
+        rs_ = pl.ds(0 if piece is None else piece * n, n)
+        if kind in (1, 2):
+            cs = pl.ds((kind - 1) * side, side)
+            src, dst = src.at[rs_, cs], dst.at[rs_, cs]
+        elif kind == 0:
+            src, dst = src.at[rs_], dst.at[rs_]
         wc[kind, slot] = send(src, dst, w_s.at[kind, slot], w_r.at[kind, slot], dev)
         sent.append(wc[kind, slot])
 
@@ -105,20 +110,20 @@
             wc[kind, slot].wait_recv()
 
     def b_first():
-        w_send(2, 0, member(), at(dx=1), first=True)
-        w_send(2, 1, member(), at(dx=-1), first=True)
-        w_send(2, 6, member(), at(dc=1), first=True)
+        w_send(3, 0, member(), at(dx=1), first=True)
+        w_send(3, 1, member(), at(dx=-1), first=True)
+        w_send(3, 6, member(), at(dc=1), first=True)
 
     def b_pass():
-        wc[2, 0].wait_recv()
-        w_send(2, 4, member(-1), at(dx=1))
-        w_send(2, 7, member(-1), at(dc=1))
-        wc[2, 1].wait_recv()
-        w_send(2, 8, member(1), at(dc=1))
+        wc[3, 0].wait_recv()
+        w_send(3, 4, member(-1), at(dx=1))
+        w_send(3, 7, member(-1), at(dc=1))
+        wc[3, 1].wait_recv()
+        w_send(3, 8, member(1), at(dc=1))
 
     def b_last():
-        wc[2, 4].wait_recv()
-        w_send(2, 9, member(2), at(dc=1))
+        wc[3, 4].wait_recv()
+        w_send(3, 9, member(2), at(dc=1))
 
     tok_send(0, 0, 0)
     tok_send(1, 0, 0)
@@ -231,18 +236,18 @@
         lax.fori_loop(0, 2, step, 0)
         y_start(g, 2 * g - 1, 2)
 
-    def decode(i, buf, lo=0, hi=8):
-        def one(j, carry):
-            q = j // 2
-            m = ((x + q + q // 2 - 2 * (q // 3)) % NX) * 2 + j % 2
+    def decode(i, buf, q):
+        cs = pl.ds(q * side, side)
+
+        def one(m, carry):
             for b in range(4):
                 r0 = pl.multiple_of((m * 4 + b) * PAD, PAD)
-                work[buf, pl.ds(r0, PAD), :] = jnp.dot(
-                    codes[i, pl.ds(r0, PAD), :], dec_all[m, pl.ds(b * 128, 128), :],
+                work[buf, pl.ds(r0, PAD), cs] = jnp.dot(
+                    codes[i, pl.ds(r0, PAD), :], dec_all[m, pl.ds(b * 128, 128), cs],
                     preferred_element_type=F32).astype(BF)
             return carry
 
-        lax.fori_loop(lo, hi, one, 0)
+        lax.fori_loop(0, 8, one, 0)
 
     def spread(i, h):
         t = jnp.concatenate([tgt[i], jnp.zeros((120, rows), F32)], axis=0)
@@ -252,66 +257,72 @@
                | ((cols[:, 2:3] == place) | (cols[:, 3:4] == place)))
         return jnp.where(hit, 1.0, 0.0).astype(BF)
 
-    def sums(h, buf, plus):
-        for j in range(4):
-            n = width // 4
-            cs = pl.ds(j * n, n)
+    def tiles(q):
+        n = side // 2
+        return [pl.ds(q * side + j * n, n) for j in range(2)]
+
+    def sums(h, buf, q, plus):
+        for cs in tiles(q):
             total = jnp.dot(sels[h], work[buf, :, cs], preferred_element_type=F32)
             for ref in plus:
                 total = total + ref[:, cs].astype(F32)
             yield cs, total
 
-    def combine(h, buf, dst, plus=()):
-        for cs, total in sums(h, buf, plus):
+    def combine(h, buf, q, dst, plus=()):
+        for cs, total in sums(h, buf, q, plus):
             dst[:, cs] = total.astype(BF)
 
     rs = {}
 
-    def rs_send(d, k, o, src):
-        rs[d, k, o] = send(src, rs_in.at[d, k, o], rs_s.at[d, k, o], rs_r.at[d, k, o],
-                           at(dz=1 if d == 0 else -1))
+    def rs_send(d, q, k, o, src):
+        cs = pl.ds(q * side, side)
+        rs[d, q, k, o] = send(src.at[:, cs], rs_in.at[d, k, o, :, cs], rs_s.at[d, q, k, o], rs_r.at[d, q, k, o],
+                              at(dz=1 if d == 0 else -1))
         if k > 1 or (k == 1 and o == 0):
-            sent.append(rs[d, k, o])
-
-    def rs_phase():
-        for d in range(2):
-            combine(d, 0, rs_first.at[d, 0])
-            rs_send(d, 0, 0, rs_first.at[d, 0])
-        for k in range(1, 4):
-            idx = (8 - 2 * k, 7 - 2 * k)
+            sent.append(rs[d, q, k, o])
+
+    def ring_start(q):
+        decode(7, 0, q)
+        for d in range(2):
+            sels[d] = spread(7, d)
+            combine(d, 0, q, rs_first.at[d, 0])
+            rs_send(d, q, 0, 0, rs_first.at[d, 0])
+        for d in range(2):
+            decode(5 + (1 - d), d, q)
+            sels[1 - d] = spread(5 + (1 - d), 1 - d)
+            combine(1 - d, d, q, rs_first.at[d, 1])
+            rs_send(d, q, 1, 1, rs_first.at[d, 1])
+
+    def ring_step(q, k):
+        idx = (8 - 2 * k, 7 - 2 * k)
+        for d in range(2):
+            if k > 1:
+                decode(idx[d], d, q)
+        for o in range(1 if k == 1 else 2):
             for d in range(2):
-                decode(idx[d], d)
-            if k == 1:
-                for d in range(2):
-                    sels[1 - d] = spread(idx[d], 1 - d)
-                    combine(1 - d, d, rs_first.at[d, 1])
-                    rs_send(d, 1, 1, rs_first.at[d, 1])
-            for o in range(2):
-                if k == 1 and o == 1:
-                    continue
-                for d in range(2):
-                    got = rs_in.at[d, k - 1, o]
-                    h = o if d == 0 else 1 - o
-                    sels[h] = spread(idx[d], h)
-                    rs[d, k - 1, o].wait_recv()
-                    combine(h, d, got, (got,))
-                    rs_send(d, k, o, got)
-        decode(0, 0)
-        for d in range(2):
-            rs[d, 0, 0].wait_send()
-            rs[d, 1, 1].wait_send()
+                got = rs_in.at[d, k - 1, o]
+                h = o if d == 0 else 1 - o
+                sels[h] = spread(idx[d], h)
+                rs[d, q, k - 1, o].wait_recv()
+                combine(h, d, q, got, (got,))
+                rs_send(d, q, k, o, got)
+
+    def ring_end(q):
+        decode(0, 0, q)
+        for d in range(2):
+            rs[d, q, 0, 0].wait_send()
+            rs[d, q, 1, 1].wait_send()
             sels[d] = spread(0, d)
         for d in range(2):
-            rs[d, 3, 0].wait_recv()
-            for cs, total in sums(d, 0, (rs_in.at[d, 3, 0], dbias)):
+            rs[d, q, 3, 0].wait_recv()
+            for cs, total in sums(d, 0, q, (rs_in.at[d, 3, 0], dbias)):
                 top = total.astype(BF)
                 rs_first[0, d, :, cs] = top
                 rs_first[1, d, :, cs] = (total - top.astype(F32)).astype(BF)
         for d in range(2):
             h = 1 - d
-            rs[d, 3, 1].wait_recv()
-            for j in range(4):
-                cs = pl.ds(j * (width // 4), width // 4)
+            rs[d, q, 3, 1].wait_recv()
+            for cs in tiles(q):
                 total = rs_first[0, h, :, cs].astype(F32) + rs_first[1, h, :, cs].astype(F32)
                 out[pl.ds(h * half, half), cs] = (total + rs_in[d, 3, 1, :, cs].astype(F32)).astype(BF)
 
@@ -329,38 +340,47 @@
     tok_pass(1, 1)
     tgt_pass(1)
     w_last(0)
-    w_done(2, (6, 7, 8, 9))
+    w_done(3, (6, 7, 8, 9))
     w_done(0, (6, 7, 8, 9, 10))
     encode(stage, 0)
     y_start(0, 0, 1)
+    w_pass(1)
+    w_first(2)
+    tok_pass(2, 0)
     staged(1)
-    tok_pass(2, 0)
     y_codes(0, 0, 1)
-    w_pass(1)
+    w_mid(1)
     staged(2)
-    y_codes(1, 1, 2)
     tok_pass(2, 1)
     tgt_pass(2)
+    y_codes(1, 1, 2)
+    w_last(1)
     staged(3)
     y_codes(2, 3, 2)
-    w_mid(1)
+    w_pass(2)
     tok[0, 3, 0].wait_recv()
     tok[1, 3, 0].wait_recv()
     tg[0, 3].wait_recv()
     encode(last, 7)
     y_start(4, 7, 1)
     y_codes(3, 5, 2)
-    for h in range(2):
-        sels[h] = spread(7, h)
+    w_mid(2)
     y_codes(4, 7, 1)
     for g in range(5):
         y_done(g)
-    w_done(1, (6, 7, 8))
-    decode(7, 0, 0, 6)
-    w_last(1)
-    w_done(1, (9, 10))
-    decode(7, 0, 6, 8)
-    rs_phase()
+    w_done(1, (6, 7, 8, 9, 10))
+    ring_start(0)
+    ring_step(0, 1)
+    w_last(2)
+    w_done(2, (6, 7, 8, 9, 10))
+    ring_step(0, 2)
+    ring_start(1)
+    ring_step(0, 3)
+    ring_step(1, 1)
+    ring_end(0)
+    ring_step(1, 2)
+    ring_step(1, 3)
+    ring_end(1)
     for copy in sent:
         copy.wait_send()
 
@@ -397,10 +417,10 @@
             pltpu.VMEM((2, 4, 2, half, width), BF),
             dma((2, 4, 2)), dma((2, 4, 2)),
             dma((2, 4)), dma((2, 4)),
-            dma((3, 11)), dma((3, 11)),
+            dma((4, 11)), dma((4, 11)),
             dma((5, 3)), dma((5, 3)),
             dma((5, 3)), dma((5, 3)),
-            dma((2, 4, 2)), dma((2, 4, 2)),
+            dma((2, 2, 4, 2)), dma((2, 2, 4, 2)),
             dma((5,)),
         ],
         compiler_params=pltpu.CompilerParams(collective_id=0, has_side_effects=True, vmem_limit_bytes=63 << 20),

time: 287 us -> 282 us (0.983)
  Pallas kernels: 281 us -> 278 us
    pallas_call x1, Pallas kernels: 281 us -> 278 us  [local(): pl.pallas_call(kernel, out_shape=(jax.ShapeDtypeStruct((rows, width), BF)...]
where the time goes in v3:
time: 282 us
  Pallas kernels  278 us (99%)
  local copies, waits for them, and re-layouts  3.53 us (1%)
    pallas_call x1, Pallas kernels, local(): pl.pallas_call(kernel, out_shape=(jax.ShapeDtypeStruct((rows, width), BF)...  278 us

profile of v3, /device:TPU:4, one launch (start us, length us, event | category | flops | bytes accessed | tf_op | source)
XLA Modules:
  0.0 281.9 jit_solution(12893840442418864877)
XLA Ops:
  0.0 0.7 fusion.4
  0.7 0.8 copy.8.table
  1.5 277.7 %encode_decode.1 = (bf16[384,2048]{1,0:T(8,128)(2,1)}, bf16[6,384,2048]{2,1,0:T(8,128)(2,1)}) custom-call(bf16[384,2048]{1,0:T(8,128)(2,1)} %tokens.1, s32[4,384]{1,0:T(4,128)} %bitcast.5, f32[256,1]{1,0:T(8,128)} %copy.8.table, bf16[2048,512]{1,0:T(8,128)(2,1)} %enc.1, f32[4,128]{1,0:T(4,128)} %bitcast.7, bf16[512,2048]{1,0:T(8,128)(2,1)} %dec.1, ...), custom_call_target="tpu_custom_call" | custom-call | tf_op jit(solution)/shard_map/encode_decode/pallas_call | solution.py:398
  279.2 2.7 copy.10

commit v4 on v3

--- a/solution.py
+++ b/solution.py
@@ -154,7 +154,7 @@
 
     base = (z * slots).astype(F32)
 
-    def encode(ref, i):
+    def gather(ref, i, buf):
         def pick(j, carry):
             n = slots // 4
             r0 = pl.multiple_of(j * n, n)
@@ -165,24 +165,27 @@
             return carry
 
         lax.fori_loop(0, 4, pick, 0)
-
-        def gather(j, carry):
-            n = width // 4
-            c0 = pl.multiple_of(j * n, n)
-            got = jnp.dot(picks[...], ref[:, pl.ds(c0, n)], preferred_element_type=F32)
-            work[0, :, pl.ds(c0, n)] = (got - dbias[:, pl.ds(c0, n)]).astype(BF)
+        for j in range(8):
+            cs = pl.ds(j * (width // 8), width // 8)
+            got = jnp.dot(picks[...], ref[:, cs], preferred_element_type=F32)
+            work[buf, :, cs] = (got - dbias[:, cs]).astype(BF)
+
+    def encode(i, n):
+        def one(j, carry):
+            for b in range(8):
+                r0 = pl.multiple_of((j * 8 + b) * PAD, PAD)
+                got = jnp.dot(work[0:n, pl.ds(r0, PAD), :].reshape(n * PAD, width),
+                              enc_all[j * 2 + b // 4, :, pl.ds(b % 4 * 128, 128)], preferred_element_type=F32)
+                for t in range(n):
+                    preact[i + t, pl.ds(r0, PAD), :] = got[t * PAD:(t + 1) * PAD]
             return carry
 
-        lax.fori_loop(0, 4, gather, 0)
-
-        def one(m, carry):
-            for b in range(4):
-                r0 = pl.multiple_of((m * 4 + b) * PAD, PAD)
-                preact[i, pl.ds(r0, PAD), :] = jnp.dot(
-                    work[0, pl.ds(r0, PAD), :], enc_all[m, :, pl.ds(b * 128, 128)], preferred_element_type=F32)
-            return carry
-
-        lax.fori_loop(0, 8, one, 0)
+        lax.fori_loop(0, 4, one, 0)
+
+    def load(i, dst, k):
+        copy = pltpu.make_async_copy(tokbuf.at[i - 1], dst, loc.at[k])
+        copy.start()
+        return copy
 
     ysum, ycode = {}, {}
 
@@ -224,18 +227,6 @@
             if k < 2 or d == 0:
                 tgt_send(d, k + 1)
 
-    def staged(g):
-        def step(j, carry):
-            i = 2 * g - 1 + j
-            copy = pltpu.make_async_copy(tokbuf.at[i - 1], stage, loc.at[4])
-            copy.start()
-            copy.wait()
-            encode(stage, i)
-            return carry
-
-        lax.fori_loop(0, 2, step, 0)
-        y_start(g, 2 * g - 1, 2)
-
     def decode(i, buf, q):
         cs = pl.ds(q * side, side)
 
@@ -332,48 +323,69 @@
     w_first(1)
     tok_pass(0, 1)
     tgt_pass(0)
+    one = load(1, out, 5)
+    for copy in local:
+        copy.wait()
+    gather(stage, 0, 0)
+    two = load(2, stage, 4)
+    one.wait()
+    gather(out, 1, 1)
     w_mid(0)
     b_last()
     tok_pass(1, 0)
-    for copy in local:
-        copy.wait()
     tok_pass(1, 1)
     tgt_pass(1)
+    three = load(3, out, 5)
     w_last(0)
     w_done(3, (6, 7, 8, 9))
     w_done(0, (6, 7, 8, 9, 10))
-    encode(stage, 0)
-    y_start(0, 0, 1)
+    encode(0, 2)
+    y_start(0, 0, 2)
     w_pass(1)
     w_first(2)
+    two.wait()
+    gather(stage, 2, 0)
+    four = load(4, stage, 4)
+    three.wait()
+    gather(out, 3, 1)
+    encode(2, 2)
     tok_pass(2, 0)
-    staged(1)
-    y_codes(0, 0, 1)
+    four.wait()
+    gather(stage, 4, 0)
+    encode(4, 1)
+    y_start(1, 2, 3)
+    y_codes(0, 0, 2)
     w_mid(1)
-    staged(2)
     tok_pass(2, 1)
     tgt_pass(2)
-    y_codes(1, 1, 2)
+    five, six = load(5, stage, 4), load(6, out, 5)
     w_last(1)
-    staged(3)
-    y_codes(2, 3, 2)
+    five.wait()
+    gather(stage, 5, 0)
+    six.wait()
+    gather(out, 6, 1)
+    encode(5, 2)
+    y_start(2, 5, 2)
+    y_codes(1, 2, 3)
     w_pass(2)
+    tg[0, 3].wait_recv()
     tok[0, 3, 0].wait_recv()
     tok[1, 3, 0].wait_recv()
-    tg[0, 3].wait_recv()
-    encode(last, 7)
-    y_start(4, 7, 1)
-    y_codes(3, 5, 2)
-    w_mid(2)
-    y_codes(4, 7, 1)
-    for g in range(5):
+    gather(last, 7, 0)
+    encode(7, 1)
+    y_start(3, 7, 1)
+    y_codes(2, 5, 2)
+    for g in range(3):
         y_done(g)
     w_done(1, (6, 7, 8, 9, 10))
+    y_codes(3, 7, 1)
+    w_mid(2)
+    y_done(3)
     ring_start(0)
     ring_step(0, 1)
     w_last(2)
+    ring_step(0, 2)
     w_done(2, (6, 7, 8, 9, 10))
-    ring_step(0, 2)
     ring_start(1)
     ring_step(0, 3)
     ring_step(1, 1)
@@ -418,10 +430,10 @@
             dma((2, 4, 2)), dma((2, 4, 2)),
             dma((2, 4)), dma((2, 4)),
             dma((4, 11)), dma((4, 11)),
-            dma((5, 3)), dma((5, 3)),
-            dma((5, 3)), dma((5, 3)),
+            dma((4, 3)), dma((4, 3)),
+            dma((4, 3)), dma((4, 3)),
             dma((2, 2, 4, 2)), dma((2, 2, 4, 2)),
-            dma((5,)),
+            dma((6,)),
         ],
         compiler_params=pltpu.CompilerParams(collective_id=0, has_side_effects=True, vmem_limit_bytes=63 << 20),
         name="encode_decode",

time: 282 us -> 274 us (0.972)
  Pallas kernels: 278 us -> 269 us
    pallas_call x1, Pallas kernels: 278 us -> 269 us  [local(): pl.pallas_call(kernel, out_shape=(jax.ShapeDtypeStruct((rows, width), BF)...]
where the time goes in v4:
time: 274 us; the launch traced here: 273 us
  Pallas kernels  269 us (98%)
  local copies, waits for them, and re-layouts  3.53 us (1%)
    pallas_call x1, Pallas kernels, local(): pl.pallas_call(kernel, out_shape=(jax.ShapeDtypeStruct((rows, width), BF)...  269 us

profile of v4, /device:TPU:4, one launch (start us, length us, event | category | flops | bytes accessed | tf_op | source)
XLA Modules:
  0.0 273.4 jit_solution(2836293507062184950)
XLA Ops:
  0.0 0.7 fusion.4
  0.7 0.8 copy.8.table
  1.5 269.2 %encode_decode.1 = (bf16[384,2048]{1,0:T(8,128)(2,1)}, bf16[6,384,2048]{2,1,0:T(8,128)(2,1)}) custom-call(bf16[384,2048]{1,0:T(8,128)(2,1)} %tokens.1, s32[4,384]{1,0:T(4,128)} %bitcast.5, f32[256,1]{1,0:T(8,128)} %copy.8.table, bf16[2048,512]{1,0:T(8,128)(2,1)} %enc.1, f32[4,128]{1,0:T(4,128)} %bitcast.7, bf16[512,2048]{1,0:T(8,128)(2,1)} %dec.1, ...), custom_call_target="tpu_custom_call" | custom-call | tf_op jit(solution)/shard_map/encode_decode/pallas_call | solution.py:410
  270.7 2.7 copy.10

commit v5 on v4

--- a/solution.py
+++ b/solution.py
@@ -165,10 +165,15 @@
             return carry
 
         lax.fori_loop(0, 4, pick, 0)
-        for j in range(8):
-            cs = pl.ds(j * (width // 8), width // 8)
-            got = jnp.dot(picks[...], ref[:, cs], preferred_element_type=F32)
-            work[buf, :, cs] = (got - dbias[:, cs]).astype(BF)
+        def product(j, carry):
+            for t in range(4):
+                n = width // 8
+                cs = pl.ds(pl.multiple_of((j * 4 + t) * n, n), n)
+                got = jnp.dot(picks[...], ref[:, cs], preferred_element_type=F32)
+                work[buf, :, cs] = (got - dbias[:, cs]).astype(BF)
+            return carry
+
+        lax.fori_loop(0, 2, product, 0)
 
     def encode(i, n):
         def one(j, carry):
@@ -272,50 +277,57 @@
         if k > 1 or (k == 1 and o == 0):
             sent.append(rs[d, q, k, o])
 
-    def ring_start(q):
+    def decode_two(i, q):
+        def one(d, carry):
+            decode(i - d, d, q)
+            return carry
+
+        lax.fori_loop(0, 2, one, 0)
+
+    def near_first(q):
+        decode_two(6, q)
+        for d in range(2):
+            sels[1 - d] = spread(6 - d, 1 - d)
+            combine(1 - d, d, q, rs_first.at[d, 1])
+            rs_send(d, q, 1, 1, rs_first.at[d, 1])
+
+    def far_first(q):
         decode(7, 0, q)
         for d in range(2):
             sels[d] = spread(7, d)
             combine(d, 0, q, rs_first.at[d, 0])
             rs_send(d, q, 0, 0, rs_first.at[d, 0])
-        for d in range(2):
-            decode(5 + (1 - d), d, q)
-            sels[1 - d] = spread(5 + (1 - d), 1 - d)
-            combine(1 - d, d, q, rs_first.at[d, 1])
-            rs_send(d, q, 1, 1, rs_first.at[d, 1])
-
-    def ring_step(q, k):
-        idx = (8 - 2 * k, 7 - 2 * k)
-        for d in range(2):
-            if k > 1:
-                decode(idx[d], d, q)
-        for o in range(1 if k == 1 else 2):
-            for d in range(2):
-                got = rs_in.at[d, k - 1, o]
-                h = o if d == 0 else 1 - o
-                sels[h] = spread(idx[d], h)
-                rs[d, q, k - 1, o].wait_recv()
-                combine(h, d, q, got, (got,))
-                rs_send(d, q, k, o, got)
-
-    def ring_end(q):
+
+    def ring_step(q, k, o):
+        decode_two(8 - 2 * k, q)
+        for d in range(2):
+            got = rs_in.at[d, k - 1, o]
+            h = o if d == 0 else 1 - o
+            sels[h] = spread(8 - 2 * k - d, h)
+            rs[d, q, k - 1, o].wait_recv()
+            combine(h, d, q, got, (got,))
+            rs_send(d, q, k, o, got)
+
+    def ring_sum(q):
         decode(0, 0, q)
         for d in range(2):
             rs[d, q, 0, 0].wait_send()
             rs[d, q, 1, 1].wait_send()
             sels[d] = spread(0, d)
         for d in range(2):
-            rs[d, q, 3, 0].wait_recv()
-            for cs, total in sums(d, 0, q, (rs_in.at[d, 3, 0], dbias)):
-                top = total.astype(BF)
-                rs_first[0, d, :, cs] = top
-                rs_first[1, d, :, cs] = (total - top.astype(F32)).astype(BF)
-        for d in range(2):
             h = 1 - d
             rs[d, q, 3, 1].wait_recv()
+            for cs, total in sums(h, 0, q, (rs_in.at[d, 3, 1], dbias)):
+                top = total.astype(BF)
+                rs_first[0, h, :, cs] = top
+                rs_first[1, h, :, cs] = (total - top.astype(F32)).astype(BF)
+
+    def ring_end(q):
+        for d in range(2):
+            rs[d, q, 3, 0].wait_recv()
             for cs in tiles(q):
-                total = rs_first[0, h, :, cs].astype(F32) + rs_first[1, h, :, cs].astype(F32)
-                out[pl.ds(h * half, half), cs] = (total + rs_in[d, 3, 1, :, cs].astype(F32)).astype(BF)
+                total = rs_first[0, d, :, cs].astype(F32) + rs_first[1, d, :, cs].astype(F32)
+                out[pl.ds(d * half, half), cs] = (total + rs_in[d, 3, 0, :, cs].astype(F32)).astype(BF)
 
     b_pass()
     tok_pass(0, 0)
@@ -367,31 +379,39 @@
     encode(5, 2)
     y_start(2, 5, 2)
     y_codes(1, 2, 3)
+    y_codes(2, 5, 2)
+    w_done(1, (6, 7, 8, 9, 10))
     w_pass(2)
+    for g in range(3):
+        y_done(g)
+    near_first(0)
     tg[0, 3].wait_recv()
     tok[0, 3, 0].wait_recv()
     tok[1, 3, 0].wait_recv()
     gather(last, 7, 0)
     encode(7, 1)
     y_start(3, 7, 1)
-    y_codes(2, 5, 2)
-    for g in range(3):
-        y_done(g)
-    w_done(1, (6, 7, 8, 9, 10))
+    w_mid(2)
     y_codes(3, 7, 1)
-    w_mid(2)
+    ring_step(0, 2, 1)
     y_done(3)
-    ring_start(0)
-    ring_step(0, 1)
+    far_first(0)
     w_last(2)
-    ring_step(0, 2)
+    ring_step(0, 3, 1)
     w_done(2, (6, 7, 8, 9, 10))
-    ring_start(1)
-    ring_step(0, 3)
-    ring_step(1, 1)
+    near_first(1)
+    far_first(1)
+    ring_step(0, 1, 0)
+    ring_step(1, 2, 1)
+    ring_step(1, 1, 0)
+    ring_step(0, 2, 0)
+    ring_step(1, 3, 1)
+    ring_step(1, 2, 0)
+    ring_sum(0)
+    ring_step(0, 3, 0)
+    ring_sum(1)
+    ring_step(1, 3, 0)
     ring_end(0)
-    ring_step(1, 2)
-    ring_step(1, 3)
     ring_end(1)
     for copy in sent:
         copy.wait_send()

time: 274 us -> 272 us (level)
  no operation moved by 1% of the time
where the time goes in v5:
time: 272 us; the launch traced here: 271 us
  Pallas kernels  267 us (98%)
  local copies, waits for them, and re-layouts  3.53 us (1%)
    pallas_call x1, Pallas kernels, local(): pl.pallas_call(kernel, out_shape=(jax.ShapeDtypeStruct((rows, width), BF)...  267 us

profile of v5, /device:TPU:4, one launch (start us, length us, event | category | flops | bytes accessed | tf_op | source)
XLA Modules:
  0.0 271.4 jit_solution(8543530673592552849)
XLA Ops:
  0.0 0.7 fusion.4
  0.7 0.8 copy.8.table
  1.5 267.2 %encode_decode.1 = (bf16[384,2048]{1,0:T(8,128)(2,1)}, bf16[6,384,2048]{2,1,0:T(8,128)(2,1)}) custom-call(bf16[384,2048]{1,0:T(8,128)(2,1)} %tokens.1, s32[4,384]{1,0:T(4,128)} %bitcast.5, f32[256,1]{1,0:T(8,128)} %copy.8.table, bf16[2048,512]{1,0:T(8,128)(2,1)} %enc.1, f32[4,128]{1,0:T(4,128)} %bitcast.7, bf16[512,2048]{1,0:T(8,128)(2,1)} %dec.1, ...), custom_call_target="tpu_custom_call" | custom-call | tf_op jit(solution)/shard_map/encode_decode/pallas_call | solution.py:430
  268.7 2.7 %copy.10 = bf16[384,2048]{1,0:T(8,128)(2,1)} copy(bf16[384,2048]{1,0:T(8,128)(2,1)} %get-tuple-element.6) | data formatting | bytes 3145728

commit v6 on v5

--- a/solution.py
+++ b/solution.py
@@ -381,10 +381,10 @@
     y_codes(1, 2, 3)
     y_codes(2, 5, 2)
     w_done(1, (6, 7, 8, 9, 10))
-    w_pass(2)
     for g in range(3):
         y_done(g)
     near_first(0)
+    w_pass(2)
     tg[0, 3].wait_recv()
     tok[0, 3, 0].wait_recv()
     tok[1, 3, 0].wait_recv()

time: 272 us -> 272 us (level)
  no operation moved by 1% of the time
where the time goes in v6:
time: 272 us; the launch traced here: 271 us
  Pallas kernels  267 us (98%)
  local copies, waits for them, and re-layouts  3.53 us (1%)
    pallas_call x1, Pallas kernels, local(): pl.pallas_call(kernel, out_shape=(jax.ShapeDtypeStruct((rows, width), BF)...  267 us

profile of v6, /device:TPU:4, one launch (start us, length us, event | category | flops | bytes accessed | tf_op | source)
XLA Modules:
  0.0 271.4 jit_solution(3689830628448492701)
XLA Ops:
  0.0 0.7 fusion.4
  0.7 0.8 copy.8.table
  1.5 267.2 %encode_decode.1 = (bf16[384,2048]{1,0:T(8,128)(2,1)}, bf16[6,384,2048]{2,1,0:T(8,128)(2,1)}) custom-call(bf16[384,2048]{1,0:T(8,128)(2,1)} %tokens.1, s32[4,384]{1,0:T(4,128)} %bitcast.5, f32[256,1]{1,0:T(8,128)} %copy.8.table, bf16[2048,512]{1,0:T(8,128)(2,1)} %enc.1, f32[4,128]{1,0:T(4,128)} %bitcast.7, bf16[512,2048]{1,0:T(8,128)(2,1)} %dec.1, ...), custom_call_target="tpu_custom_call" | custom-call | tf_op jit(solution)/shard_map/encode_decode/pallas_call | solution.py:430
  268.7 2.7 %copy.10 = bf16[384,2048]{1,0:T(8,128)(2,1)} copy(bf16[384,2048]{1,0:T(8,128)(2,1)} %get-tuple-element.6) | data formatting | bytes 3145728

commit v7 on v6

--- a/solution.py
+++ b/solution.py
@@ -393,9 +393,9 @@
     y_start(3, 7, 1)
     w_mid(2)
     y_codes(3, 7, 1)
-    ring_step(0, 2, 1)
     y_done(3)
     far_first(0)
+    ring_step(0, 2, 1)
     w_last(2)
     ring_step(0, 3, 1)
     w_done(2, (6, 7, 8, 9, 10))

time: 272 us -> 275 us (1.011)
  Pallas kernels: 267 us -> 270 us
    pallas_call x1, Pallas kernels: 267 us -> 270 us  [local(): pl.pallas_call(kernel, out_shape=(jax.ShapeDtypeStruct((rows, width), BF)...]
where the time goes in v7:
time: 275 us; the launch traced here: 274 us
  Pallas kernels  270 us (98%)
  local copies, waits for them, and re-layouts  3.53 us (1%)
    pallas_call x1, Pallas kernels, local(): pl.pallas_call(kernel, out_shape=(jax.ShapeDtypeStruct((rows, width), BF)...  270 us

profile of v7, /device:TPU:4, one launch (start us, length us, event | category | flops | bytes accessed | tf_op | source)
XLA Modules:
  0.0 274.4 jit_solution(2561490344218647030)
XLA Ops:
  0.0 0.7 fusion.4
  0.7 0.8 copy.8.table
  1.5 270.1 %encode_decode.1 = (bf16[384,2048]{1,0:T(8,128)(2,1)}, bf16[6,384,2048]{2,1,0:T(8,128)(2,1)}) custom-call(bf16[384,2048]{1,0:T(8,128)(2,1)} %tokens.1, s32[4,384]{1,0:T(4,128)} %bitcast.5, f32[256,1]{1,0:T(8,128)} %copy.8.table, bf16[2048,512]{1,0:T(8,128)(2,1)} %enc.1, f32[4,128]{1,0:T(4,128)} %bitcast.7, bf16[512,2048]{1,0:T(8,128)(2,1)} %dec.1, ...), custom_call_target="tpu_custom_call" | custom-call | tf_op jit(solution)/shard_map/encode_decode/pallas_call | solution.py:430
  271.6 2.7 copy.10
